TPU v7x, 128 devices: a whole 4x4x4 slice. The times are simulated.
128 devices in a mesh: row: 16 (over y, x), col: 8 (over z, core).
Axes of the slice: x: 4, y: 4, z: 4, core: 2. Of those that a mesh axis runs over, the one named last changes fastest.
Arguments:
- owned_rows: bfloat16 [3072, 8192], P(('row', 'col')), may hold values from -6 to 6
- suffix_lengths: int32 [128], replicated, may hold values from 1 to 24, 1024 in all
- owner_map: int32 [128], replicated, may hold values from 0 to 127, each once
- prefix_lengths: int32 [128], replicated, may hold values from 0 to 4095
- gate_weight: bfloat16 [8192, 29568], P('row', 'col'), may hold values from -0.0625 to 0.0625
- up_weight: bfloat16 [8192, 29568], P('row', 'col'), may hold values from -0.0625 to 0.0625
- down_weight: bfloat16 [29568, 8192], P('col', 'row'), may hold values from -0.03125 to 0.03125
Outputs:
- mixed: bfloat16 [1024, 8192], P('col', 'row')
Inputs may be any that keep to these rules, and one draw needn't show every extreme that they name: `suffix_lengths`: the lengths add up to 1024; the largest is exactly 24. `owner_map`: each device owns one request; request r's suffix rows fill, in order, the first suffix_lengths[r] of the 24 slots of its owner in owned_rows, and the other slots are not used.
All inputs are finite; a program needn't handle non-finite values.
Results may differ from a plain program's by a relative error of at most 0.0049.
Values may be sent and summed in bfloat16 or wider, within the bound.
No kernel may reach another device: no remote copies, remote signals or barrier semaphores. Data moves between devices by JAX's collectives and lax.ppermute only.
A program may use at most 128 MiB of HBM per device.

v0:
```python
import jax
import jax.numpy as jnp
from jax import lax
from jax.sharding import PartitionSpec as P

TOK_DEV = 8


def source_rows(suffix_lengths, owner_map, prefix_lengths, row_count, slot_size):
    request_ids = jnp.arange(suffix_lengths.shape[0], dtype=jnp.int32)
    longer = prefix_lengths[None, :] > prefix_lengths[:, None]
    earlier = (prefix_lengths[None, :] == prefix_lengths[:, None]) & (
        request_ids[None, :] < request_ids[:, None]
    )
    starts = jnp.sum(jnp.where(longer | earlier, suffix_lengths[None, :], 0), axis=1)
    positions = jnp.arange(row_count, dtype=jnp.int32)
    ends = starts + suffix_lengths
    inside = (positions[:, None] >= starts[None, :]) & (positions[:, None] < ends[None, :])
    offsets = owner_map * slot_size - starts
    shifted = jnp.sum(jnp.where(inside, offsets[None, :], 0), axis=1)
    return positions + shifted


def on_device(
    owned_rows, suffix_lengths, owner_map, prefix_lengths, gate_weight, up_weight, down_weight
):
    slot_size = owned_rows.shape[0]
    total_rows = TOK_DEV * suffix_lengths.shape[0]
    source = source_rows(suffix_lengths, owner_map, prefix_lengths, total_rows, slot_size)
    gathered = lax.all_gather(owned_rows, "col", axis=0, tiled=True)
    feature_rows = lax.all_to_all(gathered, "row", split_axis=1, concat_axis=0, tiled=True)
    suffix_rows = jnp.take(feature_rows, source, axis=0)
    block_rows = suffix_rows
    gate_share = lax.psum_scatter(
        jnp.dot(block_rows, gate_weight, preferred_element_type=jnp.float32),
        "row",
        scatter_dimension=0,
        tiled=True,
    )
    block_rows = suffix_rows
    up_share = lax.psum_scatter(
        jnp.dot(block_rows, up_weight, preferred_element_type=jnp.float32),
        "row",
        scatter_dimension=0,
        tiled=True,
    )
    hidden_share = (jax.nn.silu(gate_share) * up_share).astype(jnp.bfloat16)
    partial_sums = jnp.dot(
        lax.all_gather(hidden_share, "row", axis=0, tiled=True),
        down_weight,
        preferred_element_type=jnp.float32,
    )
    return lax.psum_scatter(partial_sums, "col", scatter_dimension=0, tiled=True).astype(
        jnp.bfloat16
    )


def solution(mesh):
    return jax.shard_map(
        on_device,
        mesh=mesh,
        in_specs=(
            P(("row", "col"), None),
            P(),
            P(),
            P(),
            P("row", "col"),
            P("row", "col"),
            P("col", "row"),
        ),
        out_specs=P("col", "row"),
        check_vma=False,
    )
```

profile of v0, /device:TPU:0, one launch (start us, length us, event | category | flops | bytes accessed | tf_op | source)
XLA Modules:
  0.0 444.5 jit_solution(16864953255005129052)
XLA Ops:
  6.5 0.0 all-gather.3.cloned.1.call-start
  6.5 0.7 all-gather.3.cloned.1.call-update
  7.3 32.2 %all-gather.3.cloned.1.call-done = bf16[192,8192]{1,0:T(8,128)(2,1)} async-done(((bf16[24,8192]{1,0:T(8,128)(2,1)}), bf16[192,8192]{1,0:T(8,128)(2,1)}) %all-gather.3.cloned.1.call-update) | async-done | bytes 3145744 | tf_op jit(solution)/shard_map/all_gather | solution.py:30
  39.5 3.9 copy.13
  43.4 0.0 copy-start.1
  43.4 0.0 copy-start.2
  43.4 6.9 %all-to-all-start = ((bf16[192,16,512]{2,0,1:T(8,128)(2,1)}), bf16[192,16,512]{2,0,1:T(8,128)(2,1)S(1)}, u32[]{:S(2)}, u32[]{:S(2)}) async-start(bf16[192,16,512]{2,0,1:T(8,128)(2,1)} %bitcast.14), calls=%async_computation | async-start | bytes 6291456 | tf_op jit(solution)/shard_map/all_to_all | solution.py:31
  50.3 0.0 reduce-scatter.6.cloned.1.call-start
  50.4 0.0 copy-done.1
  50.4 0.0 copy-done.2
  50.4 0.2 select_reduce_fusion.1
  50.6 0.0 copy-done.3
  50.6 0.2 select_reduce_fusion
  50.8 48.1 %all-to-all-done = bf16[192,16,512]{2,0,1:T(8,128)(2,1)S(1)} async-done(((bf16[192,16,512]{2,0,1:T(8,128)(2,1)}), bf16[192,16,512]{2,0,1:T(8,128)(2,1)S(1)}, u32[]{:S(2)}, u32[]{:S(2)}) %all-to-all-start) | async-done | bytes 3145760 | tf_op jit(solution)/shard_map/all_to_all | solution.py:31
  98.9 5.0 %gather_fusion = bf16[1024,512]{1,0:T(8,128)(2,1)} fusion(bf16[3072,512]{1,0:T(8,128)(2,1)S(1)} %bitcast.13, s32[1024]{0:T(1024)S(1)} %broadcast_clamp_fusion), kind=kCustom, calls=%fused_computation | custom fusion | bytes 2101248 | tf_op jit(solution)/shard_map/jit(_take)/gather | solution.py:32
  104.0 12.0 %fusion.1 = f32[1024,3696]{1,0:T(8,128)} fusion(bf16[512,3696]{0,1:T(8,128)(2,1)} %param.12, bf16[1024,512]{1,0:T(8,128)(2,1)} %gather_fusion, pred[1024]{0:T(1024)(128)(4,1)S(1)} %compare_and_fusion), kind=kOutput, calls=%fused_computation.8 | convolution fusion | flops 3876061184 | bytes 19973120 | tf_op jit(solution)/shard_map/dot_general | solution.py:42
  116.0 0.0 reduce-scatter.6.cloned.1.call-update
  116.0 0.0 reduce-scatter.4.cloned.1.call-start
  116.1 1.1 copy-done
  117.2 10.0 %fusion.2 = f32[1024,3696]{1,0:T(8,128)} fusion(bf16[512,3696]{0,1:T(8,128)(2,1)} %param.11, bf16[1024,512]{1,0:T(8,128)(2,1)S(1)} %copy-done, pred[1024]{0:T(1024)(128)(4,1)S(1)} %compare_and_fusion), kind=kOutput, calls=%fused_computation.9 | convolution fusion | flops 3876061184 | bytes 19973120 | tf_op jit(solution)/shard_map/dot_general | solution.py:35
  127.2 0.0 reduce-scatter.4.cloned.1.call-update
  127.2 0.0 all-gather.5.cloned.1.call-start
  127.3 90.2 %reduce-scatter.6.cloned.1.call-done = f32[64,3696]{1,0:T(8,128)} async-done(((f32[1024,3696]{1,0:T(8,128)}), f32[64,3696]{1,0:T(8,128)}) %reduce-scatter.6.cloned.1.call-update) | async-done | bytes 946192 | tf_op jit(solution)/shard_map/reduce_scatter | solution.py:41
  217.5 106.2 %reduce-scatter.4.cloned.1.call-done = f32[64,3696]{1,0:T(8,128)} async-done(((f32[1024,3696]{1,0:T(8,128)}), f32[64,3696]{1,0:T(8,128)}) %reduce-scatter.4.cloned.1.call-update) | async-done | bytes 946192 | tf_op jit(solution)/shard_map/reduce_scatter | solution.py:34
  323.7 2.5 multiply_convert_fusion
  326.2 0.0 all-gather.5.cloned.1.call-update
  326.2 0.0 reduce-scatter.8.cloned.1.call-start
  326.3 66.2 %all-gather.5.cloned.1.call-done = bf16[1024,3696]{1,0:T(8,128)(2,1)} async-done(((bf16[64,3696]{1,0:T(8,128)(2,1)}), bf16[1024,3696]{1,0:T(8,128)(2,1)}) %all-gather.5.cloned.1.call-update) | async-done | bytes 7569424 | tf_op jit(solution)/shard_map/all_gather | solution.py:49
  392.5 9.8 %fusion.8 = f32[1024,512]{1,0:T(8,128)} fusion(bf16[1024,3696]{1,0:T(8,128)(2,1)} %all-gather.5.cloned.1.call-done, bf16[3696,512]{1,0:T(8,128)(2,1)} %param.13), kind=kOutput, calls=%fused_computation.22 | convolution fusion | flops 3875536896 | bytes 13451264 | tf_op jit(solution)/shard_map/dot_general | solution.py:48
  402.3 0.0 reduce-scatter.8.cloned.1.call-update
  402.3 34.0 %reduce-scatter.8.cloned.1.call-done = f32[128,512]{1,0:T(8,128)} async-done(((f32[1024,512]{1,0:T(8,128)}), f32[128,512]{1,0:T(8,128)}) %reduce-scatter.8.cloned.1.call-update) | async-done | bytes 262160 | tf_op jit(solution)/shard_map/reduce_scatter | solution.py:53
  436.3 1.6 convert_element_type.7
  (6 shorter events, 0.0 us)
Async XLA Ops:
  6.5 32.9 %all-gather.3.cloned.1.call-start = ((), (), s32[]{:S(2)}) async-start(), calls=%async_computation.4 | async-start | bytes 3538944 | tf_op jit(solution)/shard_map/all_gather | solution.py:30
  43.4 7.0 %copy-start.1 = (s32[128]{0:T(128)S(1)}, s32[128]{0:T(128)}, u32[]{:S(2)}) copy-start(s32[128]{0:T(128)} %param.10) | copy-start | bytes 1540
  43.4 7.0 %copy-start.2 = (s32[128]{0:T(128)S(1)}, s32[128]{0:T(128)}, u32[]{:S(2)}) copy-start(s32[128]{0:T(128)} %param.8) | copy-start | bytes 1540
  43.4 7.2 %copy-start.3 = (s32[128]{0:T(128)S(1)}, s32[128]{0:T(128)}, u32[]{:S(2)}) copy-start(s32[128]{0:T(128)} %param.9) | copy-start | bytes 1540
  43.4 55.6 %all-to-all-start = ((bf16[192,16,512]{2,0,1:T(8,128)(2,1)}), bf16[192,16,512]{2,0,1:T(8,128)(2,1)S(1)}, u32[]{:S(2)}, u32[]{:S(2)}) async-start(bf16[192,16,512]{2,0,1:T(8,128)(2,1)} %bitcast.14), calls=%async_computation | async-start | bytes 6291456 | tf_op jit(solution)/shard_map/all_to_all | solution.py:31
  50.3 167.1 %reduce-scatter.6.cloned.1.call-start = ((), (), s32[]{:S(2)}) async-start(), calls=%async_computation.6 | async-start | bytes 16154624 | tf_op jit(solution)/shard_map/reduce_scatter | solution.py:41
  116.0 1.2 copy-start
  116.0 207.6 %reduce-scatter.4.cloned.1.call-start = ((), (), s32[]{:S(2)}) async-start(), calls=%async_computation.5 | async-start | bytes 16154624 | tf_op jit(solution)/shard_map/reduce_scatter | solution.py:34
  127.2 265.2 %all-gather.5.cloned.1.call-start = ((), (), s32[]{:S(2)}) async-start(), calls=%async_computation.7 | async-start | bytes 8077312 | tf_op jit(solution)/shard_map/all_gather | solution.py:49
  326.2 110.1 %reduce-scatter.8.cloned.1.call-start = ((), (), s32[]{:S(2)}) async-start(), calls=%async_computation.8 | async-start | bytes 2359296 | tf_op jit(solution)/shard_map/reduce_scatter | solution.py:53
Sparse Core Ops, SparseCore 0:
  9.0 30.3 all-gather.2
  116.2 101.2 reduce-scatter.5
  220.9 102.7 reduce-scatter.3
  326.4 66.0 all-gather.4
  402.5 33.8 reduce-scatter.7
where the time goes:
time: 445 us; the launch traced here: 444 us
  waiting for transfers between devices  378 us (85%)
  matrix products  31.9 us (7%)
  between operations  13.2 us (3%)
  local copies, waits for them, and re-layouts  10.1 us (2%)
  starting transfers between devices  7.11 us (2%)
  other arithmetic  4.55 us (1%)
    reduce_scatter x1, waiting for transfers between devices, on_device(): lax.psum_scatter(jnp.dot(block_rows, gate_weight, preferred_element_type=...  106 us
    reduce_scatter x1, waiting for transfers between devices, on_device(): lax.psum_scatter(jnp.dot(block_rows, up_weight, preferred_element_type=jn...  90.2 us
    all_gather x1, waiting for transfers between devices, on_device(): lax.all_gather(hidden_share, 'row', axis=0, tiled=True)  66.2 us
    all_to_all x1, waiting for transfers between devices, on_device(): lax.all_to_all(gathered, 'row', split_axis=1, concat_axis=0, tiled=True)  48.1 us
    reduce_scatter x1, waiting for transfers between devices, on_device(): lax.psum_scatter(partial_sums, 'col', scatter_dimension=0, tiled=True)  34 us
    all_gather x1, waiting for transfers between devices, on_device(): gathered = lax.all_gather(owned_rows, 'col', axis=0, tiled=True)  32.2 us
    dot_general x1, matrix products, on_device(): jnp.dot(block_rows, up_weight, preferred_element_type=jnp.float32)  12 us
    dot_general x1, matrix products, on_device(): jnp.dot(block_rows, gate_weight, preferred_element_type=jnp.float32)  9.97 us
  transfers between devices with their start and end apart: 6, of which 6 were waited for; matrix products, arithmetic and copies ran while one was open for 2% of the time, Pallas kernels for 0%

commit v1 on v0

--- a/solution.py
+++ b/solution.py
@@ -46,7 +46,9 @@
     )
     hidden_share = (jax.nn.silu(gate_share) * up_share).astype(jnp.bfloat16)
     partial_sums = jnp.dot(
-        lax.all_gather(hidden_share, "row", axis=0, tiled=True),
+        jnp.concatenate(
+            lax.all_to_all(jnp.stack([hidden_share] * lax.axis_size("row")), "row", 0, 0), axis=0
+        ),
         down_weight,
         preferred_element_type=jnp.float32,
     )

time: 445 us -> 464 us (1.043)
  blocking collectives: 0 us -> 91.8 us
  waiting for transfers between devices: 378 us -> 309 us
    all_to_all x0 -> x1, blocking collectives: none -> 91.8 us  [on_device(): lax.all_to_all(jnp.stack([hidden_share] * lax.axis_size('row')), 'row', 0...]
    all_gather x1 -> x0, waiting for transfers between devices: 66.2 us -> none  [on_device(): lax.all_gather(hidden_share, 'row', axis=0, tiled=True)]
  transfers between devices with their start and end apart: 6 -> 5, of which waited for: 6 -> 5; matrix products, arithmetic and copies ran while one was open for 2% -> 2% of each run, Pallas kernels for 0% -> 0%
where the time goes in v1:
time: 464 us
  waiting for transfers between devices  309 us (67%)
  blocking collectives  91.8 us (20%)
  matrix products  27.6 us (6%)
  between operations  13.2 us (3%)
  local copies, waits for them, and re-layouts  10.9 us (2%)
  starting transfers between devices  7.07 us (2%)
    reduce_scatter x1, waiting for transfers between devices, on_device(): lax.psum_scatter(jnp.dot(block_rows, gate_weight, preferred_element_type=...  106 us
    all_to_all x1, blocking collectives, on_device(): lax.all_to_all(jnp.stack([hidden_share] * lax.axis_size('row')), 'row', 0...  91.8 us
    reduce_scatter x1, waiting for transfers between devices, on_device(): lax.psum_scatter(jnp.dot(block_rows, up_weight, preferred_element_type=jn...  90.2 us
    all_to_all x1, waiting for transfers between devices, on_device(): lax.all_to_all(gathered, 'row', split_axis=1, concat_axis=0, tiled=True)  48.1 us
    all_gather x1, waiting for transfers between devices, on_device(): gathered = lax.all_gather(owned_rows, 'col', axis=0, tiled=True)  32.2 us
    reduce_scatter x1, waiting for transfers between devices, on_device(): lax.psum_scatter(partial_sums, 'col', scatter_dimension=0, tiled=True)  31.7 us
    dot_general x1, matrix products, on_device(): jnp.dot(block_rows, up_weight, preferred_element_type=jnp.float32)  12 us
    dot_general x1, matrix products, on_device(): jnp.dot(block_rows, gate_weight, preferred_element_type=jnp.float32)  9.97 us
  transfers between devices with their start and end apart: 5, of which 5 were waited for; matrix products, arithmetic and copies ran while one was open for 2% of the time, Pallas kernels for 0%

profile of v1, /device:TPU:0, one launch (start us, length us, event | category | flops | bytes accessed | tf_op | source)
XLA Modules:
  0.0 463.7 jit_solution(7950284538344193213)
XLA Ops:
  6.5 0.0 all-gather.2.cloned.1.call-start
  6.5 0.7 all-gather.2.cloned.1.call-update
  7.3 32.2 %all-gather.2.cloned.1.call-done = bf16[192,8192]{1,0:T(8,128)(2,1)} async-done(((bf16[24,8192]{1,0:T(8,128)(2,1)}), bf16[192,8192]{1,0:T(8,128)(2,1)}) %all-gather.2.cloned.1.call-update) | async-done | bytes 3145744 | tf_op jit(solution)/shard_map/all_gather | solution.py:30
  39.5 3.9 copy.13
  43.4 0.0 copy-start.1
  43.4 6.9 %all-to-all-start = ((bf16[192,16,512]{2,0,1:T(8,128)(2,1)}), bf16[192,16,512]{2,0,1:T(8,128)(2,1)S(1)}, u32[]{:S(2)}, u32[]{:S(2)}) async-start(bf16[192,16,512]{2,0,1:T(8,128)(2,1)} %bitcast.15), calls=%async_computation | async-start | bytes 6291456 | tf_op jit(solution)/shard_map/all_to_all | solution.py:31
  50.3 0.0 reduce-scatter.6.cloned.1.call-start
  50.4 0.0 copy-done.1
  50.4 0.0 copy-done.2
  50.4 0.2 select_reduce_fusion.1
  50.6 0.0 copy-done.3
  50.6 0.2 select_reduce_fusion
  50.8 48.1 %all-to-all-done = bf16[192,16,512]{2,0,1:T(8,128)(2,1)S(1)} async-done(((bf16[192,16,512]{2,0,1:T(8,128)(2,1)}), bf16[192,16,512]{2,0,1:T(8,128)(2,1)S(1)}, u32[]{:S(2)}, u32[]{:S(2)}) %all-to-all-start) | async-done | bytes 3145760 | tf_op jit(solution)/shard_map/all_to_all | solution.py:31
  98.9 5.0 %gather_fusion = bf16[1024,512]{1,0:T(8,128)(2,1)} fusion(bf16[3072,512]{1,0:T(8,128)(2,1)S(1)} %bitcast.14, s32[1024]{0:T(1024)S(1)} %broadcast_clamp_fusion), kind=kCustom, calls=%fused_computation | custom fusion | bytes 2101248 | tf_op jit(solution)/shard_map/jit(_take)/gather | solution.py:32
  104.0 12.0 %fusion.1 = f32[1024,3696]{1,0:T(8,128)} fusion(bf16[512,3696]{0,1:T(8,128)(2,1)} %param.12, bf16[1024,512]{1,0:T(8,128)(2,1)} %gather_fusion, pred[1024]{0:T(1024)(128)(4,1)S(1)} %compare_and_fusion), kind=kOutput, calls=%fused_computation.8 | convolution fusion | flops 3876061184 | bytes 19973120 | tf_op jit(solution)/shard_map/dot_general | solution.py:42
  116.0 0.0 reduce-scatter.6.cloned.1.call-update
  116.0 0.0 reduce-scatter.4.cloned.1.call-start
  116.1 1.1 copy-done
  117.2 10.0 %fusion.2 = f32[1024,3696]{1,0:T(8,128)} fusion(bf16[512,3696]{0,1:T(8,128)(2,1)} %param.11, bf16[1024,512]{1,0:T(8,128)(2,1)S(1)} %copy-done, pred[1024]{0:T(1024)(128)(4,1)S(1)} %compare_and_fusion), kind=kOutput, calls=%fused_computation.9 | convolution fusion | flops 3876061184 | bytes 19973120 | tf_op jit(solution)/shard_map/dot_general | solution.py:35
  127.2 0.0 reduce-scatter.4.cloned.1.call-update
  127.2 0.0 reduce-scatter.8.cloned.1.call-start
  127.3 90.2 %reduce-scatter.6.cloned.1.call-done = f32[64,3696]{1,0:T(8,128)} async-done(((f32[1024,3696]{1,0:T(8,128)}), f32[64,3696]{1,0:T(8,128)}) %reduce-scatter.6.cloned.1.call-update) | async-done | bytes 946192 | tf_op jit(solution)/shard_map/reduce_scatter | solution.py:41
  217.5 106.4 %reduce-scatter.4.cloned.1.call-done = f32[64,3696]{1,0:T(8,128)} async-done(((f32[1024,3696]{1,0:T(8,128)}), f32[64,3696]{1,0:T(8,128)}) %reduce-scatter.4.cloned.1.call-update) | async-done | bytes 946192 | tf_op jit(solution)/shard_map/reduce_scatter | solution.py:34
  323.8 1.7 multiply_convert_fusion
  325.6 0.8 stack.2
  326.4 0.0 copy-start.4
  326.4 91.8 %all_to_all.24 = bf16[16,64,3696]{2,1,0:T(8,128)(2,1)S(1)} all-to-all(bf16[16,64,3696]{2,1,0:T(8,128)(2,1)S(1)} %stack.2), channel_id=1, replica_groups=mesh['row'=16,'col'=8] {'row'}, dimensions={0} | all-to-all | bytes 15138816 | tf_op jit(solution)/shard_map/all_to_all | solution.py:50
  418.2 0.0 copy-done.4
  418.2 5.6 %fusion.8 = f32[1024,512]{1,0:T(8,128)} fusion(bf16[1024,3696]{1,0:T(8,128)(2,1)S(1)} %bitcast.16, bf16[3696,512]{1,0:T(8,128)(2,1)S(1)} %copy-done.4), kind=kOutput, calls=%fused_computation.22 | convolution fusion | flops 3875536896 | bytes 13451264 | tf_op jit(solution)/shard_map/dot_general | solution.py:48
  423.8 0.0 reduce-scatter.8.cloned.1.call-update
  423.8 31.7 %reduce-scatter.8.cloned.1.call-done = f32[128,512]{1,0:T(8,128)} async-done(((f32[1024,512]{1,0:T(8,128)}), f32[128,512]{1,0:T(8,128)}) %reduce-scatter.8.cloned.1.call-update) | async-done | bytes 262160 | tf_op jit(solution)/shard_map/reduce_scatter | solution.py:55
  455.5 1.6 convert_element_type.7
  (7 shorter events, 0.0 us)
Async XLA Ops:
  6.5 32.9 %all-gather.2.cloned.1.call-start = ((), (), s32[]{:S(2)}) async-start(), calls=%async_computation.5 | async-start | bytes 3538944 | tf_op jit(solution)/shard_map/all_gather | solution.py:30
  43.4 7.0 %copy-start.1 = (s32[128]{0:T(128)S(1)}, s32[128]{0:T(128)}, u32[]{:S(2)}) copy-start(s32[128]{0:T(128)} %param.10) | copy-start | bytes 1540
  43.4 7.0 %copy-start.2 = (s32[128]{0:T(128)S(1)}, s32[128]{0:T(128)}, u32[]{:S(2)}) copy-start(s32[128]{0:T(128)} %param.8) | copy-start | bytes 1540
  43.4 7.2 %copy-start.3 = (s32[128]{0:T(128)S(1)}, s32[128]{0:T(128)}, u32[]{:S(2)}) copy-start(s32[128]{0:T(128)} %param.9) | copy-start | bytes 1540
  43.4 55.6 %all-to-all-start = ((bf16[192,16,512]{2,0,1:T(8,128)(2,1)}), bf16[192,16,512]{2,0,1:T(8,128)(2,1)S(1)}, u32[]{:S(2)}, u32[]{:S(2)}) async-start(bf16[192,16,512]{2,0,1:T(8,128)(2,1)} %bitcast.15), calls=%async_computation | async-start | bytes 6291456 | tf_op jit(solution)/shard_map/all_to_all | solution.py:31
  50.3 167.2 %reduce-scatter.6.cloned.1.call-start = ((), (), s32[]{:S(2)}) async-start(), calls=%async_computation.7 | async-start | bytes 16154624 | tf_op jit(solution)/shard_map/reduce_scatter | solution.py:41
  116.0 1.2 copy-start
  116.0 207.8 %reduce-scatter.4.cloned.1.call-start = ((), (), s32[]{:S(2)}) async-start(), calls=%async_computation.6 | async-start | bytes 16154624 | tf_op jit(solution)/shard_map/reduce_scatter | solution.py:34
  127.2 328.3 %reduce-scatter.8.cloned.1.call-start = ((), (), s32[]{:S(2)}) async-start(), calls=%async_computation.8 | async-start | bytes 2359296 | tf_op jit(solution)/shard_map/reduce_scatter | solution.py:55
  326.4 91.9 %copy-start.4 = (bf16[3696,512]{1,0:T(8,128)(2,1)S(1)}, bf16[3696,512]{1,0:T(8,128)(2,1)}, u32[]{:S(2)}) copy-start(bf16[3696,512]{1,0:T(8,128)(2,1)} %param.13) | copy-start | bytes 11354116
Sparse Core Ops, SparseCore 0:
  9.0 30.3 all-gather.1
  116.1 101.2 reduce-scatter.5
  220.9 102.8 reduce-scatter.3
  423.9 31.5 reduce-scatter.7
